TPU v7x, 128 devices: a whole 4x4x4 slice. The times are simulated.
128 devices in a mesh: grp: 4 (over x_hi, core), dom: 32 (over z, y, x_lo).
Axes of the slice: x: 4 (x_hi: 2, x_lo: 2; x = x_hi * 2 + x_lo), y: 4, z: 4, core: 2. Of those that a mesh axis runs over, the one named last changes fastest.
Arguments:
- nodes: bfloat16 [131072, 256], P(('grp', 'dom')), may hold values from -8 to 8
- neighbours: int32 [131072, 8], P(('grp', 'dom')), may hold values from 0 to 1279
- send_rows: int32 [32768], P(('grp', 'dom')), may hold values from 0 to 1023
- landmark_ids: int32 [8192], P(('grp', 'dom')), may hold values from 0 to 1023
- w_dst: bfloat16 [256, 256], replicated, may hold values from -0.375 to 0.375
- w_src: bfloat16 [256, 256], replicated, may hold values from -0.375 to 0.375
- w_msg: bfloat16 [256, 256], replicated, may hold values from -0.375 to 0.375
- edge_bias: float32 [256], replicated, may hold values from -4 to 4
- w_query: bfloat16 [256, 256], replicated, may hold values from -0.375 to 0.375
- w_key: bfloat16 [256, 256], replicated, may hold values from -0.375 to 0.375
- w_value: bfloat16 [256, 256], replicated, may hold values from -0.375 to 0.375
- w_out: bfloat16 [256, 256], replicated, may hold values from -0.375 to 0.375
Outputs:
- result: bfloat16 [131072, 256], P(('grp', 'dom'))
- kernel_term: float32 [131072, 256], P(('grp', 'dom'))
Inputs may be any that keep to these rules, and one draw needn't show every extreme that they name: `neighbours`: entries index the device's own 1024 rows, then the 128 rows received from the previous partition, then the 128 rows from the next one. `send_rows`: each partition's entries are rows of its own nodes. `landmark_ids`: each partition's entries are rows of its own nodes.
All inputs are finite; a program needn't handle non-finite values.
Results may differ from a plain program's by a relative error of at most 0.0054.
Values may be sent and summed in bfloat16 or wider, within the bound.
A program may use at most 64 MiB of HBM per device.

v0:
```python
import math
import jax
import jax.numpy as jnp
from jax import lax
from jax.sharding import PartitionSpec as P


def extended_2(cells, sides, width):
    for axis, dim in sides:
        count = lax.axis_size(axis)
        head = lax.slice_in_dim(cells, 0, width, axis=dim)
        tail = lax.slice_in_dim(cells, cells.shape[dim] - width, cells.shape[dim], axis=dim)
        cells = jnp.concatenate(
            [
                lax.ppermute(tail, axis, [(i, (i + 1) % count) for i in range(count)]),
                cells,
                lax.ppermute(head, axis, [((i + 1) % count, i) for i in range(count)]),
            ],
            axis=dim,
        )
    return cells


def rms_scale(values):
    return values * lax.rsqrt(jnp.mean(values * values, axis=-1, keepdims=True) + 1e-06)


def kernel_tile(query, key_rows):
    scale = 2.0 * query.shape[1] ** (-0.5)
    return jnp.exp(jnp.dot(query, key_rows.T, preferred_element_type=jnp.float32) * scale).astype(
        jnp.bfloat16
    )


def partial_sums(query, value, key_rows):
    total_rows = key_rows.shape[0]
    block_size = math.gcd(total_rows, 512)
    blocks = key_rows.reshape(total_rows // block_size, block_size, key_rows.shape[1])

    def partial_one_block(block_keys):
        kernel = kernel_tile(query, block_keys)
        return lax.dot_general(
            kernel, value, (((0,), (0,)), ((), ())), preferred_element_type=jnp.float32
        )

    return lax.map(partial_one_block, blocks).reshape(total_rows, value.shape[1])


def apply_sums(query, key_rows, sum_rows):
    total_rows = key_rows.shape[0]
    block_size = math.gcd(total_rows, 512)
    key_blocks = key_rows.reshape(total_rows // block_size, block_size, key_rows.shape[1])
    sum_blocks = sum_rows.reshape(total_rows // block_size, block_size, sum_rows.shape[1])

    def apply_one_block(accum, pair):
        block_keys, block_sums = pair
        kernel = kernel_tile(query, block_keys)
        return (accum + jnp.dot(kernel, block_sums, preferred_element_type=jnp.float32), None)

    start_value = jnp.zeros((query.shape[0], sum_rows.shape[1]), jnp.float32)
    accum, _ = lax.scan(apply_one_block, start_value, (key_blocks, sum_blocks))
    return accum


def shards(
    nodes,
    neighbours,
    send_rows,
    landmark_ids,
    w_dst,
    w_src,
    w_msg,
    edge_bias,
    w_query,
    w_key,
    w_value,
    w_out,
):
    halo_count = send_rows.shape[0] // 2
    outgoing = jnp.concatenate(
        [nodes[send_rows[:halo_count]], nodes[send_rows[halo_count:]]], axis=0
    )
    padded = extended_2(outgoing, ((("grp", "dom"), 0),), halo_count)
    extended = jnp.concatenate([nodes, padded[:halo_count], padded[3 * halo_count :]], axis=0)
    source = jnp.dot(extended, w_src, preferred_element_type=jnp.float32)
    target = jnp.dot(nodes, w_dst, preferred_element_type=jnp.float32)
    preact = target[:, None, :] + source[neighbours] + edge_bias
    messages = jnp.mean(jax.nn.gelu(preact), axis=1).astype(jnp.bfloat16)
    updated = (
        nodes.astype(jnp.float32) + jnp.dot(messages, w_msg, preferred_element_type=jnp.float32)
    ).astype(jnp.bfloat16)
    normed = rms_scale(updated.astype(jnp.float32)).astype(jnp.bfloat16)
    query = jnp.dot(normed, w_query, preferred_element_type=jnp.float32).astype(jnp.bfloat16)
    value = jnp.dot(normed, w_value, preferred_element_type=jnp.float32).astype(jnp.bfloat16)
    local_keys = jnp.dot(normed[landmark_ids], w_key, preferred_element_type=jnp.float32).astype(
        jnp.bfloat16
    )
    all_keys = lax.all_gather(local_keys, ("grp", "dom"), axis=0, tiled=True)
    own_sums = partial_sums(query, value, all_keys)
    total_sums = lax.psum(own_sums, ("grp", "dom")).astype(jnp.bfloat16)
    smooth = apply_sums(query, all_keys, total_sums)
    kernel_term = rms_scale(smooth)
    scaled = kernel_term.astype(jnp.bfloat16)
    result = updated.astype(jnp.float32) + jnp.dot(
        scaled, w_out, preferred_element_type=jnp.float32
    )
    return (result.astype(jnp.bfloat16), kernel_term)


def solution(mesh):
    return jax.shard_map(
        shards,
        mesh=mesh,
        in_specs=(
            P(("grp", "dom"), None),
            P(("grp", "dom"), None),
            P(("grp", "dom")),
            P(("grp", "dom")),
            P(),
            P(),
            P(),
            P(),
            P(),
            P(),
            P(),
            P(),
        ),
        out_specs=(P(("grp", "dom"), None), P(("grp", "dom"), None)),
        check_vma=False,
    )
```

profile of v0, /device:TPU:0, one launch (start us, length us, event | category | flops | bytes accessed | tf_op | source)
XLA Modules:
  0.0 572.5 jit_solution(5054479233434508780)
XLA Ops:
  7.2 0.0 all-gather.2.cloned.1.call-start
  7.2 0.8 compare_select_fusion.3
  8.0 1.9 gather_fusion
  9.9 1.6 collective-permute-start
  11.5 1.9 gather_fusion.1
  13.4 6.7 %collective-permute-start.1 = (bf16[128,256]{1,0:T(8,128)(2,1)S(1)}, bf16[128,256]{1,0:T(8,128)(2,1)}, u32[]{:S(2)}, u32[]{:S(2)}) collective-permute-start(bf16[128,256]{1,0:T(8,128)(2,1)S(1)} %gather_fusion.1), channel_id=1, source_target_pairs={{1,0},{2,1},{3,2},{4,3},{5,4},{6,5},{7,6},{8,7},{9,8},{10,9},{11,1... | collective-permute-start | bytes 196616 | tf_op jit(solution)/shard_map/ppermute | solution.py:17
  20.1 1.2 copy.18
  21.4 0.8 compare_select_fusion
  22.1 0.2 copy.19
  22.3 0.3 reshape.53
  22.6 1.4 fusion.46
  24.0 0.7 compare_select_fusion.1
  24.6 0.6 copy-done.7
  25.3 1.4 fusion.36
  26.7 31.6 %gather_fusion.2 = f32[8192,256]{1,0:T(8,128)} fusion(f32[1280,256]{1,0:T(8,128)S(1)} %fusion.36, s32[8192]{0:T(1024)S(1)} %broadcast_clamp_fusion), kind=kCustom, calls=%fused_computation.2 | custom fusion | bytes 16809984 | tf_op jit(solution)/shard_map/gather | solution.py:87
  58.3 7.8 %fusion.30 = f32[1024,256]{1,0:T(8,128)S(1)} fusion(f32[8192,256]{1,0:T(8,128)} %gather_fusion.2, f32[256]{0:T(256)S(1)} %copy-done.8, f32[1024,256]{1,0:T(8,128)S(1)} %fusion.46), kind=kLoop, calls=%fused_computation.31 | loop fusion | flops 22806528 | bytes 10486784 | tf_op jit(solution)/shard_map/reduce_sum | solution.py:88
  66.2 0.4 fusion.34
  66.6 0.1 fusion.35
  66.7 0.2 copy.20
  66.9 0.7 gather_fusion.3
  67.6 0.8 convolution_convert_fusion.2
  68.4 0.0 all-gather.2.cloned.1.call-update
  68.5 0.4 convolution_convert_fusion.1
  68.8 0.4 convolution_convert_fusion
  69.2 302.4 %all-gather.2.cloned.1.call-done = bf16[8192,256]{1,0:T(8,128)(2,1)} async-done(((bf16[64,256]{1,0:T(8,128)(2,1)}), bf16[8192,256]{1,0:T(8,128)(2,1)}) %all-gather.2.cloned.1.call-update) | async-done | bytes 4194320 | tf_op jit(solution)/shard_map/all_gather | solution.py:98
  371.6 41.7 %while.21 = (s32[]{:T(128)}, f32[16,512,256]{2,1,0:T(8,128)}, bf16[16,512,256]{2,1,0:T(8,128)(2,1)}, bf16[1024,256]{1,0:T(8,128)(2,1)S(1)}, bf16[1024,256]{1,0:T(8,128)(2,1)S(1)}, /*index=5*/s32[]{:T(128)}) while((s32[]{:T(128)}, f32[16,512,256]{2,1,0:T(8,128)}, bf16[16,512,256]{2,1,0:T(8,128)(2,1)}, bf16[1024,256]{1,0:T(8,128)(2,1)S(1)}, ...), condition=%wide.region_3.4_spmd, body=%wide.region_2.3_spmd.sunk | while | flops 537919488 | bytes 1836101 | solution.py:46
  371.6 2.6 fusion.72
  374.2 2.6 fusion.72
  376.8 2.6 fusion.72
  379.4 2.6 fusion.72
  382.0 2.6 fusion.72
  384.6 2.6 fusion.72
  387.2 2.6 fusion.72
  389.8 2.6 fusion.72
  392.4 2.6 fusion.72
  395.0 2.6 fusion.72
  397.6 2.6 fusion.72
  400.2 2.6 fusion.72
  402.8 2.6 fusion.72
  405.4 2.6 fusion.72
  408.0 2.6 fusion.72
  410.6 2.6 fusion.72
  413.3 114.5 %all-reduce.1 = bf16[8192,256]{1,0:T(8,128)(2,1)} all-reduce(f32[8192,256]{1,0:T(8,128)} %bitcast.52), channel_id=1, replica_groups=mesh['grp'=4,'dom'=32] {'grp','dom'}, use_global_device_ids=true, to_apply=%region_4.5 | all-reduce | flops 2097152 | bytes 12582912 | tf_op jit(solution)/shard_map/psum | solution.py:100
  527.7 36.1 %while.22 = (s32[]{:T(128)}, f32[1024,256]{1,0:T(8,128)S(1)}, bf16[16,512,256]{2,1,0:T(8,128)(2,1)}, bf16[1024,256]{1,0:T(8,128)(2,1)S(1)}, bf16[16,512,256]{2,1,0:T(8,128)(2,1)}, /*index=5*/s32[]{:T(128)}, s32[]{:T(128)}) while((s32[]{:T(128)}, f32[1024,256]{1,0:T(8,128)S(1)}, bf16[16,512,256]{2,1,0:T(8,128)(2,1)}, ...), condition=%wide.region_6.7_spmd.clone, body=%wide.region_5.6_spmd.clone.sunk | while | flops 538443776 | bytes 3146839 | solution.py:61
  527.7 2.3 fusion.76
  530.0 2.2 fusion.76
  532.3 2.2 fusion.76
  534.5 2.2 fusion.76
  536.8 2.2 fusion.76
  539.0 2.2 fusion.76
  541.3 2.2 fusion.76
  543.5 2.2 fusion.76
  545.8 2.2 fusion.76
  548.0 2.2 fusion.76
  550.3 2.2 fusion.76
  552.5 2.2 fusion.76
  554.8 2.2 fusion.76
  557.1 2.2 fusion.76
  559.3 2.2 fusion.76
  561.6 2.2 fusion.76
  563.8 0.2 multiply_reduce_fusion
  564.0 0.2 broadcast_multiply_fusion
  564.3 0.3 fusion.32
  564.6 1.0 copy.22
  (27 shorter events, 0.1 us)
Async XLA Ops:
  7.2 18.1 %copy-start = (bf16[256,256]{1,0:T(8,128)(2,1)S(1)}, bf16[256,256]{1,0:T(8,128)(2,1)}, u32[]{:S(2)}) copy-start(bf16[256,256]{1,0:T(8,128)(2,1)} %param.21) | copy-start | bytes 393220
  7.2 364.4 %all-gather.2.cloned.1.call-start = ((), (), s32[]{:S(2)}) async-start(), calls=%async_computation | async-start | bytes 4227072 | tf_op jit(solution)/shard_map/all_gather | solution.py:98
  9.9 14.8 %collective-permute-start = (bf16[128,256]{1,0:T(8,128)(2,1)S(1)}, bf16[128,256]{1,0:T(8,128)(2,1)S(1)}, u32[]{:S(2)}, u32[]{:S(2)}) collective-permute-start(bf16[128,256]{1,0:T(8,128)(2,1)S(1)} %gather_fusion), channel_id=1, source_target_pairs={{0,1},{1,2},{2,3},{3,4},{4,5},{5,6},{6,7},{7,8},{8,9},{9,10},{10,1... | collective-permute-start | bytes 196616 | tf_op jit(solution)/shard_map/ppermute | solution.py:15
  13.4 11.9 %collective-permute-start.1 = (bf16[128,256]{1,0:T(8,128)(2,1)S(1)}, bf16[128,256]{1,0:T(8,128)(2,1)}, u32[]{:S(2)}, u32[]{:S(2)}) collective-permute-start(bf16[128,256]{1,0:T(8,128)(2,1)S(1)} %gather_fusion.1), channel_id=1, source_target_pairs={{1,0},{2,1},{3,2},{4,3},{5,4},{6,5},{7,6},{8,7},{9,8},{10,9},{11,1... | collective-permute-start | bytes 196616 | tf_op jit(solution)/shard_map/ppermute | solution.py:17
  24.6 0.6 copy-start.7
  26.7 31.6 %copy-start.8 = (f32[256]{0:T(256)S(1)}, f32[256]{0:T(256)}, u32[]{:S(2)}) copy-start(f32[256]{0:T(256)} %param.23) | copy-start | bytes 3076
  58.3 7.9 %copy-start.2 = (bf16[256,256]{1,0:T(8,128)(2,1)S(1)}, bf16[256,256]{1,0:T(8,128)(2,1)}, u32[]{:S(2)}) copy-start(bf16[256,256]{1,0:T(8,128)(2,1)} %param.22) | copy-start | bytes 393220
  58.3 9.3 %copy-start.6 = (bf16[256,256]{1,0:T(8,128)(2,1)S(1)}, bf16[256,256]{1,0:T(8,128)(2,1)}, u32[]{:S(2)}) copy-start(bf16[256,256]{1,0:T(8,128)(2,1)} %param.25) | copy-start | bytes 393220
  58.3 10.1 %copy-start.3 = (bf16[256,256]{1,0:T(8,128)(2,1)S(1)}, bf16[256,256]{1,0:T(8,128)(2,1)}, u32[]{:S(2)}) copy-start(bf16[256,256]{1,0:T(8,128)(2,1)} %param.24) | copy-start | bytes 393220
  58.3 10.5 %copy-start.4 = (bf16[256,256]{1,0:T(8,128)(2,1)S(1)}, bf16[256,256]{1,0:T(8,128)(2,1)}, u32[]{:S(2)}) copy-start(bf16[256,256]{1,0:T(8,128)(2,1)} %param.26) | copy-start | bytes 393220
  527.7 36.5 %copy-start.5 = (bf16[256,256]{1,0:T(8,128)(2,1)S(1)}, bf16[256,256]{1,0:T(8,128)(2,1)}, u32[]{:S(2)}) copy-start(bf16[256,256]{1,0:T(8,128)(2,1)} %param.27) | copy-start | bytes 393220
  564.3 1.4 copy-start.1
Sparse Core Ops, SparseCore 0:
  68.6 302.9 all-gather.1
where the time goes:
time: 574 us; the launch traced here: 572 us
  waiting for transfers between devices  302 us (53%)
  blocking collectives  114 us (20%)
  matrix products  82.4 us (14%)
  local copies, waits for them, and re-layouts  39.6 us (7%)
  between operations  14.3 us (2%)
  other arithmetic  10.6 us (2%)
  starting transfers between devices  8.41 us (1%)
    all_gather x1, waiting for transfers between devices, shards(): all_keys = lax.all_gather(local_keys, ('grp', 'dom'), axis=0, tiled=True)  302 us
    psum x1, blocking collectives, shards(): total_sums = lax.psum(own_sums, ('grp', 'dom')).astype(jnp.bfloat16)  114 us
    dot_general x16, matrix products, partial_one_block(): lax.dot_general(kernel, value, (((0,), (0,)), ((), ())), preferred_elemen...  41.7 us
    dot_general x16, matrix products, apply_one_block(): jnp.dot(kernel, block_sums, preferred_element_type=jnp.float32)  35.7 us
    gather x1, local copies, waits for them, and re-layouts, shards(): preact = target[:, None, :] + source[neighbours] + edge_bias  31.6 us
  transfers between devices with their start and end apart: 3, of which 1 were waited for; matrix products, arithmetic and copies ran while one was open for 1% of the time, Pallas kernels for 0%

commit v1 on v0

--- a/solution.py
+++ b/solution.py
@@ -95,7 +95,10 @@
     local_keys = jnp.dot(normed[landmark_ids], w_key, preferred_element_type=jnp.float32).astype(
         jnp.bfloat16
     )
-    all_keys = lax.all_gather(local_keys, ("grp", "dom"), axis=0, tiled=True)
+    size = lax.axis_size(("grp", "dom"))
+    pieces = jnp.stack([local_keys for _ in range(size)])
+    pieces = lax.all_to_all(pieces, ("grp", "dom"), split_axis=0, concat_axis=0)
+    all_keys = jnp.concatenate(pieces, axis=0)
     own_sums = partial_sums(query, value, all_keys)
     total_sums = lax.psum(own_sums, ("grp", "dom")).astype(jnp.bfloat16)
     smooth = apply_sums(query, all_keys, total_sums)

time: 574 us -> 315 us (0.55)
  waiting for transfers between devices: 302 us -> 52 us
  between operations: 14.3 us -> 0.88 us
  starting transfers between devices: 8.41 us -> 15 us
    all_gather x1 -> x0, waiting for transfers between devices: 302 us -> none  [shards(): all_keys = lax.all_gather(local_keys, ('grp', 'dom'), axis=0, tiled=True)]
    all_to_all x0 -> x1, waiting for transfers between devices: none -> 52 us  [shards(): pieces = lax.all_to_all(pieces, ('grp', 'dom'), split_axis=0, concat_axis=0)]
    all_to_all x0 -> x1, starting transfers between devices: none -> 6.61 us  [shards(): pieces = lax.all_to_all(pieces, ('grp', 'dom'), split_axis=0, concat_axis=0)]
  transfers between devices with their start and end apart: 3 -> 3, of which waited for: 1 -> 1; matrix products, arithmetic and copies ran while one was open for 1% -> 2% of each run, Pallas kernels for 0% -> 0%
where the time goes in v1:
time: 315 us; the launch traced here: 314 us
  blocking collectives  111 us (35%)
  matrix products  81.7 us (26%)
  waiting for transfers between devices  52 us (17%)
  local copies, waits for them, and re-layouts  41.9 us (13%)
  starting transfers between devices  15 us (5%)
  other arithmetic  10.5 us (3%)
    psum x1, blocking collectives, shards(): total_sums = lax.psum(own_sums, ('grp', 'dom')).astype(jnp.bfloat16)  111 us
    all_to_all x1, waiting for transfers between devices, shards(): pieces = lax.all_to_all(pieces, ('grp', 'dom'), split_axis=0, concat_axis=0)  52 us
    dot_general x16, matrix products, partial_one_block(): lax.dot_general(kernel, value, (((0,), (0,)), ((), ())), preferred_elemen...  41.6 us
    dot_general x16, matrix products, apply_one_block(): jnp.dot(kernel, block_sums, preferred_element_type=jnp.float32)  35.7 us
    gather x1, local copies, waits for them, and re-layouts, shards(): preact = target[:, None, :] + source[neighbours] + edge_bias  31.4 us
    reduce_sum x1, other arithmetic, shards(): messages = jnp.mean(jax.nn.gelu(preact), axis=1).astype(jnp.bfloat16)  7.74 us
    ppermute x1, starting transfers between devices, extended_2(): lax.ppermute(head, axis, [((i + 1) % count, i) for i in range(count)])  6.72 us
    all_to_all x1, starting transfers between devices, shards(): pieces = lax.all_to_all(pieces, ('grp', 'dom'), split_axis=0, concat_axis=0)  6.61 us
  transfers between devices with their start and end apart: 3, of which 1 were waited for; matrix products, arithmetic and copies ran while one was open for 2% of the time, Pallas kernels for 0%

profile of v1, /device:TPU:0, one launch (start us, length us, event | category | flops | bytes accessed | tf_op | source)
XLA Modules:
  0.0 313.6 jit_solution(11008944966914575057)
XLA Ops:
  0.6 0.8 compare_select_fusion.3
  1.4 1.9 gather_fusion
  3.3 1.6 collective-permute-start
  4.9 1.9 gather_fusion.1
  6.8 6.7 %collective-permute-start.1 = (bf16[128,256]{1,0:T(8,128)(2,1)S(1)}, bf16[128,256]{1,0:T(8,128)(2,1)}, u32[]{:S(2)}, u32[]{:S(2)}) collective-permute-start(bf16[128,256]{1,0:T(8,128)(2,1)S(1)} %gather_fusion.1), channel_id=1, source_target_pairs={{1,0},{2,1},{3,2},{4,3},{5,4},{6,5},{7,6},{8,7},{9,8},{10,9},{11,1... | collective-permute-start | bytes 196616 | tf_op jit(solution)/shard_map/ppermute | solution.py:17
  13.5 1.2 copy.18
  14.8 0.8 compare_select_fusion
  15.5 0.2 copy.19
  15.7 0.3 reshape.50
  16.0 1.4 fusion.46
  17.4 0.7 compare_select_fusion.1
  18.1 0.6 copy-done.7
  18.7 1.4 fusion.36
  20.1 31.4 %gather_fusion.2 = f32[8192,256]{1,0:T(8,128)} fusion(f32[1280,256]{1,0:T(8,128)S(1)} %fusion.36, s32[8192]{0:T(1024)S(1)} %broadcast_clamp_fusion), kind=kCustom, calls=%fused_computation.2 | custom fusion | bytes 16809984 | tf_op jit(solution)/shard_map/gather | solution.py:87
  51.6 7.7 %fusion.30 = f32[1024,256]{1,0:T(8,128)S(1)} fusion(f32[8192,256]{1,0:T(8,128)} %gather_fusion.2, f32[256]{0:T(256)S(1)} %copy-done.8, f32[1024,256]{1,0:T(8,128)S(1)} %fusion.46), kind=kLoop, calls=%fused_computation.31 | loop fusion | flops 22806528 | bytes 10486784 | tf_op jit(solution)/shard_map/reduce_sum | solution.py:88
  59.3 0.4 fusion.34
  59.8 0.1 fusion.35
  59.9 0.2 copy.20
  60.1 0.7 gather_fusion.3
  60.8 0.1 convolution_convert_fusion.2
  60.9 2.5 stack.2
  63.4 6.6 %all-to-all-start = ((bf16[128,64,256]{2,1,0:T(8,128)(2,1)}), bf16[128,64,256]{2,1,0:T(8,128)(2,1)}, u32[]{:S(2)}, u32[]{:S(2)}) async-start(bf16[128,64,256]{2,1,0:T(8,128)(2,1)} %stack.2), calls=%async_computation | async-start | bytes 8388608 | tf_op jit(solution)/shard_map/all_to_all | solution.py:100
  70.1 0.4 convolution_convert_fusion.1
  70.4 0.4 convolution_convert_fusion
  70.8 52.0 %all-to-all-done = bf16[128,64,256]{2,1,0:T(8,128)(2,1)} async-done(((bf16[128,64,256]{2,1,0:T(8,128)(2,1)}), bf16[128,64,256]{2,1,0:T(8,128)(2,1)}, u32[]{:S(2)}, u32[]{:S(2)}) %all-to-all-start) | async-done | bytes 4194336 | tf_op jit(solution)/shard_map/all_to_all | solution.py:100
  122.8 41.6 %while.21 = (s32[]{:T(128)}, f32[16,512,256]{2,1,0:T(8,128)}, bf16[16,512,256]{2,1,0:T(8,128)(2,1)}, bf16[1024,256]{1,0:T(8,128)(2,1)S(1)}, bf16[1024,256]{1,0:T(8,128)(2,1)S(1)}, /*index=5*/s32[]{:T(128)}) while((s32[]{:T(128)}, f32[16,512,256]{2,1,0:T(8,128)}, bf16[16,512,256]{2,1,0:T(8,128)(2,1)}, bf16[1024,256]{1,0:T(8,128)(2,1)S(1)}, ...), condition=%wide.region_3.4_spmd, body=%wide.region_2.3_spmd.sunk | while | flops 537919488 | bytes 1836101 | solution.py:46
  122.8 2.6 fusion.72
  125.4 2.6 fusion.72
  128.0 2.6 fusion.72
  130.6 2.6 fusion.72
  133.2 2.6 fusion.72
  135.8 2.6 fusion.72
  138.4 2.6 fusion.72
  141.0 2.6 fusion.72
  143.6 2.6 fusion.72
  146.2 2.6 fusion.72
  148.8 2.6 fusion.72
  151.4 2.6 fusion.72
  154.0 2.6 fusion.72
  156.6 2.6 fusion.72
  159.2 2.6 fusion.72
  161.8 2.6 fusion.72
  164.4 111.3 %all-reduce.1 = bf16[8192,256]{1,0:T(8,128)(2,1)} all-reduce(f32[8192,256]{1,0:T(8,128)} %bitcast.52), channel_id=1, replica_groups=mesh['grp'=4,'dom'=32] {'grp','dom'}, use_global_device_ids=true, to_apply=%region_4.5 | all-reduce | flops 2097152 | bytes 12582912 | tf_op jit(solution)/shard_map/psum | solution.py:103
  275.7 36.1 %while.22 = (s32[]{:T(128)}, f32[1024,256]{1,0:T(8,128)S(1)}, bf16[16,512,256]{2,1,0:T(8,128)(2,1)}, bf16[1024,256]{1,0:T(8,128)(2,1)S(1)}, bf16[16,512,256]{2,1,0:T(8,128)(2,1)}, /*index=5*/s32[]{:T(128)}, s32[]{:T(128)}) while((s32[]{:T(128)}, f32[1024,256]{1,0:T(8,128)S(1)}, bf16[16,512,256]{2,1,0:T(8,128)(2,1)}, ...), condition=%wide.region_6.7_spmd.clone, body=%wide.region_5.6_spmd.clone.sunk | while | flops 538443776 | bytes 3146839 | solution.py:61
  275.7 2.3 fusion.76
  278.0 2.2 fusion.76
  280.3 2.2 fusion.76
  282.5 2.2 fusion.76
  284.8 2.2 fusion.76
  287.0 2.2 fusion.76
  289.3 2.2 fusion.76
  291.5 2.2 fusion.76
  293.8 2.2 fusion.76
  296.0 2.2 fusion.76
  298.3 2.2 fusion.76
  300.5 2.2 fusion.76
  302.8 2.2 fusion.76
  305.1 2.2 fusion.76
  307.3 2.2 fusion.76
  309.6 2.2 fusion.76
  311.8 0.2 multiply_reduce_fusion
  312.0 0.2 broadcast_multiply_fusion
  312.3 0.3 fusion.32
  312.6 1.0 copy.22
  (27 shorter events, 0.1 us)
Async XLA Ops:
  0.6 18.1 %copy-start = (bf16[256,256]{1,0:T(8,128)(2,1)S(1)}, bf16[256,256]{1,0:T(8,128)(2,1)}, u32[]{:S(2)}) copy-start(bf16[256,256]{1,0:T(8,128)(2,1)} %param.21) | copy-start | bytes 393220
  3.3 14.8 %collective-permute-start = (bf16[128,256]{1,0:T(8,128)(2,1)S(1)}, bf16[128,256]{1,0:T(8,128)(2,1)S(1)}, u32[]{:S(2)}, u32[]{:S(2)}) collective-permute-start(bf16[128,256]{1,0:T(8,128)(2,1)S(1)} %gather_fusion), channel_id=1, source_target_pairs={{0,1},{1,2},{2,3},{3,4},{4,5},{5,6},{6,7},{7,8},{8,9},{9,10},{10,1... | collective-permute-start | bytes 196616 | tf_op jit(solution)/shard_map/ppermute | solution.py:15
  6.8 11.9 %collective-permute-start.1 = (bf16[128,256]{1,0:T(8,128)(2,1)S(1)}, bf16[128,256]{1,0:T(8,128)(2,1)}, u32[]{:S(2)}, u32[]{:S(2)}) collective-permute-start(bf16[128,256]{1,0:T(8,128)(2,1)S(1)} %gather_fusion.1), channel_id=1, source_target_pairs={{1,0},{2,1},{3,2},{4,3},{5,4},{6,5},{7,6},{8,7},{9,8},{10,9},{11,1... | collective-permute-start | bytes 196616 | tf_op jit(solution)/shard_map/ppermute | solution.py:17
  18.0 0.6 copy-start.7
  20.1 31.4 %copy-start.8 = (f32[256]{0:T(256)S(1)}, f32[256]{0:T(256)}, u32[]{:S(2)}) copy-start(f32[256]{0:T(256)} %param.23) | copy-start | bytes 3076
  51.6 7.8 %copy-start.2 = (bf16[256,256]{1,0:T(8,128)(2,1)S(1)}, bf16[256,256]{1,0:T(8,128)(2,1)}, u32[]{:S(2)}) copy-start(bf16[256,256]{1,0:T(8,128)(2,1)} %param.22) | copy-start | bytes 393220
  51.6 9.2 %copy-start.6 = (bf16[256,256]{1,0:T(8,128)(2,1)S(1)}, bf16[256,256]{1,0:T(8,128)(2,1)}, u32[]{:S(2)}) copy-start(bf16[256,256]{1,0:T(8,128)(2,1)} %param.25) | copy-start | bytes 393220
  59.3 10.7 %copy-start.3 = (bf16[256,256]{1,0:T(8,128)(2,1)S(1)}, bf16[256,256]{1,0:T(8,128)(2,1)}, u32[]{:S(2)}) copy-start(bf16[256,256]{1,0:T(8,128)(2,1)} %param.24) | copy-start | bytes 393220
  59.7 10.7 %copy-start.4 = (bf16[256,256]{1,0:T(8,128)(2,1)S(1)}, bf16[256,256]{1,0:T(8,128)(2,1)}, u32[]{:S(2)}) copy-start(bf16[256,256]{1,0:T(8,128)(2,1)} %param.26) | copy-start | bytes 393220
  63.4 59.4 %all-to-all-start = ((bf16[128,64,256]{2,1,0:T(8,128)(2,1)}), bf16[128,64,256]{2,1,0:T(8,128)(2,1)}, u32[]{:S(2)}, u32[]{:S(2)}) async-start(bf16[128,64,256]{2,1,0:T(8,128)(2,1)} %stack.2), calls=%async_computation | async-start | bytes 8388608 | tf_op jit(solution)/shard_map/all_to_all | solution.py:100
  275.7 36.5 %copy-start.5 = (bf16[256,256]{1,0:T(8,128)(2,1)S(1)}, bf16[256,256]{1,0:T(8,128)(2,1)}, u32[]{:S(2)}) copy-start(bf16[256,256]{1,0:T(8,128)(2,1)} %param.27) | copy-start | bytes 393220
  312.3 1.4 copy-start.1
